TPU v7x, 32 devices: a whole 2x2x4 slice. The times are simulated.
32 devices in a mesh: space: 4 (over y, x), mode: 8 (over z, core).
Axes of the slice: x: 2, y: 2, z: 4, core: 2. Of those that a mesh axis runs over, the one named last changes fastest.
Arguments:
- source_field: float32 [8, 4, 128, 2048], P('space', None, None, 'mode'), may hold values from -6 to 6
- mean_operator: float32 [8, 4, 128, 896], P('space'), may hold values from -0.109375 to 0.109375
- field_operators: float32 [4, 8, 4, 128, 896], P(None, 'space'), may hold values from -0.078125 to 0.078125
- adjacency: int32 [8, 4, 4], P('space'), may hold values from 0 to 3
- mode_masks: int32 [4], replicated, may hold values from 256 to 1024, as said below
Outputs:
- solution_field: float32 [8, 4, 128, 2048], P('space', None, None, 'mode')
- residual: float32 [8, 4, 128, 2048], P('space', None, None, 'mode')
Inputs may be any that keep to these rules, and one draw needn't show every extreme that they name: `mode_masks`: each value is 256 times a power of two, at most 1024, and every such value belongs to at least one field.
All inputs are finite; a program needn't handle non-finite values.
Results may differ from a plain program's by a relative error of at most 0.0001.
Values sent between devices are 32-bit elements; how exact they have to be, the bound alone decides.
A program may use at most 128 MiB of HBM per device.

v0:
```python
import functools

import jax
import jax.numpy as jnp
from jax import lax
from jax.experimental import pallas as pl
from jax.experimental.pallas import tpu as pltpu
from jax.sharding import PartitionSpec as P

DEGREE = 4
COUPLING = 0.5773502691896258
THETA = 1.0
DELTA = 0.7
CHUNKS = 4
GROUP = 2
LAG = 2
SLOTS = 4
Y_FIRST = True
VMEM_LIMIT = 66_000_000
MESH = pl.DeviceIdType.MESH


def prepare(raw, e, slot, modes_dev, adj_ref, mask_ref, w_hi, w_lo):
    face, blk = w_hi.shape[1], raw.shape[2]
    layer, f = e // face, lax.rem(e, face)
    for op in range(w_hi.shape[3] // blk):
        if op == 0:
            weights = [None]
        else:
            weights = [
                jnp.where(mask_ref[j] == modes_dev * (1 << (op - 1)), COUPLING, 0.0).astype(jnp.float32)
                for j in range(raw.shape[1] - 1)
            ]

        def block(s):
            lanes = slice(s * blk, (s + 1) * blk)
            if op == 0:
                return raw[slot, 0, :, lanes]
            total = weights[0] * raw[slot, 1, :, lanes]
            for j in range(1, len(weights)):
                total = total + weights[j] * raw[slot, 1 + j, :, lanes]
            return total

        own = block(0)
        sides = [block(3 + s) for s in range(adj_ref.shape[2])]
        parts = []
        for g in range(face):
            total = jnp.where(f == g, 1.0, 0.0).astype(jnp.float32) * own
            for s, side in enumerate(sides):
                total = total + jnp.where(adj_ref[layer, f, s] == g, 1.0, 0.0).astype(jnp.float32) * side
            parts.append(total)
        parts += [block(1), block(2)]
        for at, part in enumerate(parts):
            part = part.T
            high = part.astype(jnp.bfloat16)
            low = (part - high.astype(jnp.float32)).astype(jnp.bfloat16)
            w_hi[layer, f, at * blk : (at + 1) * blk, op * blk : (op + 1) * blk] = high
            w_lo[layer, f, at * blk : (at + 1) * blk, op * blk : (op + 1) * blk] = low


def solve_kernel(
    peers, spaces, chunks, modes_dev, src, mean, fields, adj, masks, x_out, r_out,
    raw, w_hi, w_lo, direction, res, x, split, halo_low, halo_up, relay,
    w_sem, own_sem, in_send, in_recv, low_send, low_recv, up_send, up_recv,
    relay_send, relay_recv, forward_send, forward_recv, out_send, out_recv, own_out,
):
    layers, face = w_hi.shape[:2]
    blk = w_hi.shape[3] // (peers.bit_length())
    bits = peers.bit_length() - 1
    lc = src.shape[3]
    rows = peers * lc
    me = lax.axis_index("mode")
    s = lax.axis_index("space")
    has_low = s > 0
    has_up = s < spaces - 1
    relayed = spaces >= 4 and spaces % 2 == 0
    odd = lax.rem(s, 2) == 1
    even = jnp.logical_not(odd)
    half = rows // 2 if relayed else rows

    elements = layers * face

    def loads(e):
        slot = lax.rem(e, SLOTS)
        l, f = e // face, lax.rem(e, face)
        return (
            pltpu.make_async_copy(mean.at[l, f], raw.at[slot, 0], w_sem.at[slot, 0]),
            pltpu.make_async_copy(fields.at[:, l, f], raw.at[slot, pl.ds(1, fields.shape[0])], w_sem.at[slot, 1]),
        )

    for e in range(min(SLOTS, elements)):
        for load in loads(e):
            load.start()

    barrier = pltpu.get_barrier_semaphore()
    for k in range(1, peers):
        pl.semaphore_signal(barrier, inc=1, device_id={"mode": lax.rem(me + k, peers)}, device_id_type=MESH)

    @pl.when(has_low)
    def _():
        pl.semaphore_signal(barrier, inc=1, device_id={"space": s - 1}, device_id_type=MESH)

    @pl.when(has_up)
    def _():
        pl.semaphore_signal(barrier, inc=1, device_id={"space": s + 1}, device_id_type=MESH)

    expected = peers - 1 + has_low.astype(jnp.int32) + has_up.astype(jnp.int32)
    if relayed:
        far_low, far_up = s >= 2, s < spaces - 2
        expected = expected + far_low.astype(jnp.int32) + far_up.astype(jnp.int32)

        @pl.when(far_low)
        def _():
            pl.semaphore_signal(barrier, inc=1, device_id={"space": s - 2}, device_id_type=MESH)

        @pl.when(far_up)
        def _():
            pl.semaphore_signal(barrier, inc=1, device_id={"space": s + 2}, device_id_type=MESH)

    pl.semaphore_wait(barrier, expected)

    def slab(ref, c, h):
        return ref.at[c, :, pl.ds(pl.multiple_of(h * lc, lc), lc), :]

    def in_copy(c, k):
        to = lax.rem(me + k, peers)
        return pltpu.make_async_remote_copy(
            src_ref=src.at[to, c], dst_ref=slab(direction.at[0], c, me),
            send_sem=in_send.at[c, k], recv_sem=in_recv.at[c, k],
            device_id={"mode": to}, device_id_type=MESH,
        )

    def in_wait(c, k):
        pltpu.make_async_remote_copy(
            src_ref=src.at[0, c], dst_ref=slab(direction.at[0], c, lax.rem(me + peers - k, peers)),
            send_sem=in_send.at[c, k], recv_sem=in_recv.at[c, k],
            device_id={"mode": lax.rem(me + k, peers)}, device_id_type=MESH,
        ).wait_recv()

    def own_copy(c):
        return pltpu.make_async_copy(src.at[me, c], slab(direction.at[0], c, me), own_sem.at[c])

    def to_low(t, c, count):
        return pltpu.make_async_remote_copy(
            src_ref=direction.at[lax.rem(t, 2), c, 0, pl.ds(0, count)], dst_ref=halo_up.at[t, c, pl.ds(0, count)],
            send_sem=low_send.at[t, c], recv_sem=up_recv.at[t, c],
            device_id={"space": s - 1}, device_id_type=MESH,
        )

    def to_up(t, c, count):
        return pltpu.make_async_remote_copy(
            src_ref=direction.at[lax.rem(t, 2), c, layers - 1, pl.ds(0, count)],
            dst_ref=halo_low.at[t, c, pl.ds(0, count)],
            send_sem=up_send.at[t, c], recv_sem=low_recv.at[t, c],
            device_id={"space": s + 1}, device_id_type=MESH,
        )

    def to_relay(t, c, layer, offset):
        return pltpu.make_async_remote_copy(
            src_ref=direction.at[lax.rem(t, 2), c, layer, pl.ds(half, rows - half)], dst_ref=relay.at[t, c],
            send_sem=relay_send.at[t, c], recv_sem=relay_recv.at[t, c],
            device_id={"space": s + offset}, device_id_type=MESH,
        )

    def forward(t, c, halo, offset):
        return pltpu.make_async_remote_copy(
            src_ref=relay.at[t, c], dst_ref=halo.at[t, c, pl.ds(half, rows - half)],
            send_sem=forward_send.at[t, c], recv_sem=forward_recv.at[t, c],
            device_id={"space": s + offset}, device_id_type=MESH,
        )

    both = jnp.logical_and
    up_offset, low_offset = (2, -2) if Y_FIRST else (-1, 1)
    if relayed:
        whole_low, whole_up = both(odd, has_low), both(even, has_up)
        part_low, part_up = both(even, has_low), both(odd, has_up)
    else:
        whole_low, whole_up = has_low, has_up

    def halo_each(t, c, act):
        @pl.when(whole_low)
        def _():
            act(to_low(t, c, rows))

        @pl.when(whole_up)
        def _():
            act(to_up(t, c, rows))

        if relayed:

            @pl.when(part_low)
            def _():
                act(to_relay(t, c, 0, low_offset))
                act(to_low(t, c, half))

            @pl.when(part_up)
            def _():
                act(to_relay(t, c, layers - 1, up_offset))
                act(to_up(t, c, half))

    def halo_start(t, c):
        halo_each(t, c, lambda copy: copy.start())

    def halo_sent(t, c):
        halo_each(t, c, lambda copy: copy.wait_send())

    def forward_each(t, c, act):
        if relayed:

            @pl.when(both(odd, s >= 3))
            def _():
                act(forward(t, c, *((halo_low, -1) if Y_FIRST else (halo_up, -2))))

            @pl.when(both(even, s < spaces - 3))
            def _():
                act(forward(t, c, *((halo_up, 1) if Y_FIRST else (halo_low, 2))))

    def halo_forward(t, c):
        if relayed:

            @pl.when(jnp.logical_or(both(odd, s >= 3), both(even, s < spaces - 3)))
            def _():
                to_relay(t, c, 0, jnp.where(odd, -1, 1)).wait_recv()

            forward_each(t, c, lambda copy: copy.start())

    def halo_arrived(t, c):
        if not relayed:

            @pl.when(has_low)
            def _():
                to_up(t, c, rows).wait_recv()

            @pl.when(has_up)
            def _():
                to_low(t, c, rows).wait_recv()

            return

        @pl.when(both(odd, has_low))
        def _():
            to_up(t, c, rows).wait_recv()

        @pl.when(both(even, has_up))
        def _():
            to_low(t, c, rows).wait_recv()

        @pl.when(both(even, has_low))
        def _():
            to_up(t, c, half).wait_recv()
            forward(t, c, halo_low, -1).wait_recv()

        @pl.when(both(odd, has_up))
        def _():
            to_low(t, c, half).wait_recv()
            forward(t, c, halo_up, 1).wait_recv()

    def out_copy(which, ref, out, c, k):
        to = lax.rem(me + k, peers)
        return pltpu.make_async_remote_copy(
            src_ref=slab(ref, c, to), dst_ref=out.at[me, c],
            send_sem=out_send.at[which, c, k], recv_sem=out_recv.at[which, c, k],
            device_id={"mode": to}, device_id_type=MESH,
        )

    def out_own(which, ref, out, c):
        return pltpu.make_async_copy(slab(ref, c, me), out.at[me, c], own_out.at[which, c])

    def out_start(which, ref, out, c):
        for k in range(1, peers):
            out_copy(which, ref, out, c, k).start()
        out_own(which, ref, out, c).start()

    def out_finish(which, ref, out, c):
        for k in range(1, peers):
            came = lax.rem(me + peers - k, peers)
            out_copy(which, ref, out, c, k).wait_send()
            pltpu.make_async_remote_copy(
                src_ref=slab(ref, c, me), dst_ref=out.at[came, c],
                send_sem=out_send.at[which, c, k], recv_sem=out_recv.at[which, c, k],
                device_id={"mode": lax.rem(me + k, peers)}, device_id_type=MESH,
            ).wait_recv()
        out_own(which, ref, out, c).wait()

    for c in range(chunks):
        for k in range(1, peers):
            in_copy(c, k).start()
        own_copy(c).start()

    @pl.when(jnp.logical_not(has_low))
    def _():
        halo_low[...] = jnp.zeros_like(halo_low)

    @pl.when(jnp.logical_not(has_up))
    def _():
        halo_up[...] = jnp.zeros_like(halo_up)

    def arrive(c):
        own_copy(c).wait()
        for k in range(1, peers):
            in_wait(c, k)
        halo_start(0, c)
        res[c] = direction[0, c]
        x[c] = direction[0, c]

    def build(e, carry):
        for load in loads(e):
            load.wait()
        prepare(raw, e, lax.rem(e, SLOTS), modes_dev, adj, masks, w_hi, w_lo)

        @pl.when(e + SLOTS < elements)
        def _():
            for load in loads(e + SLOTS):
                load.start()

        @pl.when(e == elements // 2)
        def _():
            arrive(0)

        return carry

    lax.fori_loop(0, elements, build, 0)
    group = min(GROUP, chunks)
    for c in range(1, group):
        arrive(c)

    def keep_split(at, value):
        high = value.astype(jnp.bfloat16)
        split[at, :rows, :] = high
        split[at, rows:, :] = (value - high.astype(jnp.float32)).astype(jnp.bfloat16)

    def product(a, b):
        return lax.dot_general(a, b, (((1,), (0,)), ((), ())), preferred_element_type=jnp.float32)

    sigma = THETA / DELTA

    ratios = [1.0 / sigma]
    for _ in range(DEGREE):
        ratios.append(1.0 / (2.0 * sigma - ratios[-1]))
    order = []
    arrivals = {}
    for turn in range(DEGREE + LAG * (chunks // group - 1)):
        for place in range(group):
            for c in range(place, chunks, group):
                t = turn - LAG * (c // group)
                if 0 <= t < DEGREE:
                    order.append((t, c))
        for c in range(group, chunks):
            if turn == max(LAG * (c // group) - 1, 0):
                arrivals[c] = len(order) - 1


    def step(i, carry):
        t, c = jnp.int32(0), jnp.int32(0)
        for at, (t_at, c_at) in enumerate(order):
            t = jnp.where(i == at, t_at, t)
            c = jnp.where(i == at, c_at, c)
        now = lax.rem(t, 2)
        keep, add = jnp.float32(0.0), jnp.float32(0.0)
        for at in range(DEGREE):
            keep = jnp.where(t == at, jnp.float32(ratios[at + 1] * ratios[at]), keep)
            add = jnp.where(t == at, jnp.float32(2.0 * ratios[at + 1] / DELTA), add)
        for l in range(layers):
            keep_split(l + 1, direction[now, c, l])
        halo_forward(t, c)
        halo_arrived(t, c)
        keep_split(0, halo_low[t, c])
        keep_split(layers + 1, halo_up[t, c])

        @pl.when(t > 0)
        def _():
            halo_sent(t - 1, c)

        for l in range(layers):
            for f in range(face):
                lanes = slice(f * blk, (f + 1) * blk)
                a = jnp.concatenate([split[l + 1], split[l, :, lanes], split[l + 2, :, lanes]], axis=1)
                y = product(a, w_hi[l, f])
                y = y[:rows] + y[rows:] + product(a[:rows], w_lo[l, f])
                d = direction[now, c, l, :, lanes]
                total = d + y[:, :blk]
                for b in range(bits):
                    term = y[:, (b + 1) * blk : (b + 2) * blk]
                    total = total + jnp.concatenate(
                        [term[(h ^ (1 << b)) * lc : ((h ^ (1 << b)) + 1) * lc] for h in range(peers)], axis=0
                    )
                r = res[c, l, :, lanes] - total
                res[c, l, :, lanes] = r

                @pl.when(t < DEGREE - 1)
                def _():
                    d_new = keep * d + add * r
                    direction[1 - now, c, l, :, lanes] = d_new
                    x[c, l, :, lanes] = x[c, l, :, lanes] + d_new

        @pl.when(t < DEGREE - 1)
        def _():
            halo_start(t + 1, c)

        @pl.when(t == DEGREE - 2)
        def _():
            out_start(0, x, x_out, c)

        @pl.when(t == DEGREE - 1)
        def _():
            out_start(1, res, r_out, c)

        for late, at in arrivals.items():

            @pl.when(i == at)
            def _():
                arrive(late)

        return carry

    lax.fori_loop(0, DEGREE * chunks, step, 0)

    for c in range(chunks):
        halo_sent(DEGREE - 1, c)
        for t in range(DEGREE):
            forward_each(t, c, lambda copy: copy.wait_send())
        for k in range(1, peers):
            in_copy(c, k).wait_send()
    for c in range(chunks):
        out_finish(0, x, x_out, c)
        out_finish(1, res, r_out, c)


def per_device(peers, spaces, source_field, mean_operator, field_operators, adjacency, mode_masks):
    layers, face, blk, modes_dev = source_field.shape
    bits = peers.bit_length() - 1
    chunks = CHUNKS
    while modes_dev % (peers * chunks * 8):
        chunks //= 2
    lc = modes_dev // (peers * chunks)
    rows = peers * lc
    wide = face * blk
    weights = pltpu.VMEM((layers, face, (face + 2) * blk, (bits + 1) * blk), jnp.bfloat16)
    src = source_field.reshape(layers, face, blk, peers, chunks, lc)
    src = src.transpose(3, 4, 0, 5, 1, 2).reshape(peers, chunks, layers, lc, wide) / THETA
    out = jax.ShapeDtypeStruct(src.shape, jnp.float32)
    field = pltpu.VMEM((chunks, layers, rows, wide), jnp.float32)
    halo = pltpu.VMEM((DEGREE, chunks, rows, wide), jnp.float32)
    dma = pltpu.SemaphoreType.DMA
    x, r = pl.pallas_call(
        functools.partial(solve_kernel, peers, spaces, chunks, modes_dev),
        in_specs=[
            pl.BlockSpec(memory_space=pltpu.VMEM),
            pl.BlockSpec(memory_space=pl.ANY),
            pl.BlockSpec(memory_space=pl.ANY),
            pl.BlockSpec(memory_space=pltpu.SMEM),
            pl.BlockSpec(memory_space=pltpu.SMEM),
        ],
        out_specs=(pl.BlockSpec(memory_space=pl.ANY), pl.BlockSpec(memory_space=pl.ANY)),
        out_shape=(out, out),
        scratch_shapes=[
            pltpu.VMEM((SLOTS, 1 + field_operators.shape[0]) + mean_operator.shape[2:], jnp.float32),
            weights,
            weights,
            pltpu.VMEM((2, chunks, layers, rows, wide), jnp.float32),
            field,
            field,
            pltpu.VMEM((layers + 2, 2 * rows, wide), jnp.bfloat16),
            halo,
            halo,
            pltpu.VMEM((DEGREE, chunks, rows // 2, wide), jnp.float32),
            dma((SLOTS, 2)),
            dma((chunks,)),
            dma((chunks, peers)),
            dma((chunks, peers)),
            dma((DEGREE, chunks)),
            dma((DEGREE, chunks)),
            dma((DEGREE, chunks)),
            dma((DEGREE, chunks)),
            dma((DEGREE, chunks)),
            dma((DEGREE, chunks)),
            dma((DEGREE, chunks)),
            dma((DEGREE, chunks)),
            dma((2, chunks, peers)),
            dma((2, chunks, peers)),
            dma((2, chunks)),
        ],
        compiler_params=pltpu.CompilerParams(
            collective_id=0, has_side_effects=True, vmem_limit_bytes=VMEM_LIMIT
        ),
    )(src, mean_operator, field_operators, adjacency, mode_masks)

    def back(value):
        value = value.reshape(peers, chunks, layers, lc, face, blk)
        return value.transpose(2, 4, 5, 0, 1, 3).reshape(layers, face, blk, modes_dev)

    return back(x), back(r)


def solution(mesh):
    in_specs = (
        P("space", None, None, "mode"),
        P("space", None, None, None),
        P(None, "space", None, None, None),
        P("space", None, None),
        P(),
    )
    out_specs = (P("space", None, None, "mode"), P("space", None, None, "mode"))
    return jax.shard_map(
        functools.partial(per_device, mesh.shape["mode"], mesh.shape["space"]),
        mesh=mesh, in_specs=in_specs, out_specs=out_specs, check_vma=False,
    )
```

profile of v0, /device:TPU:5, one launch (start us, length us, event | category | flops | bytes accessed | tf_op | source)
XLA Modules:
  0.0 124.3 jit_solution(5050326728101110632)
XLA Ops:
  0.6 1.5 %copy.10 = f32[2,4,128,256]{2,3,1,0:T(8,128)S(1)} copy(f32[2,4,128,256]{3,2,1,0:T(8,128)} %param.5) | data formatting | bytes 2097152 | tf_op args[0]
  2.2 1.1 copy.17
  3.3 115.7 %shard_map.68 = (f32[8,4,2,8,512]{4,3,2,1,0:T(8,128)}, f32[8,4,2,8,512]{4,3,2,1,0:T(8,128)}) custom-call(f32[8,4,2,8,512]{4,3,2,1,0:T(8,128)} %bitcast.14, f32[2,4,128,896]{3,2,1,0:T(8,128)} %mean.1, f32[4,2,4,128,896]{4,3,2,1,0:T(8,128)} %fields.1, s32[2,4,4]{2,1,0:T(4,128)} %adj.1, s32[4]{0:T(128)} %masks.1), custom_call_target="tpu_custom_call" | custom-call | tf_op jit(solution)/shard_map/pallas_call | solution.py:445
  119.0 1.4 %copy.12 = f32[8,4,2,8,4,128]{5,3,1,0,4,2:T(8,128)S(1)} copy(f32[8,4,2,8,4,128]{5,3,4,2,1,0:T(8,128)} %bitcast.19) | data formatting | bytes 2097152 | tf_op jit(solution)/shard_map/reshape | solution.py:489
  120.3 1.3 %copy.14 = f32[2,4,128,256]{3,2,1,0:T(8,128)} copy(f32[2,4,128,256]{2,3,1,0:T(8,128)S(1)} %bitcast.15) | data formatting | bytes 2097152
  121.7 1.4 %copy.13 = f32[8,4,2,8,4,128]{5,3,1,0,4,2:T(8,128)S(1)} copy(f32[8,4,2,8,4,128]{5,3,4,2,1,0:T(8,128)} %bitcast.18) | data formatting | bytes 2097152 | tf_op jit(solution)/shard_map/reshape | solution.py:489
  123.0 1.3 %copy.15 = f32[2,4,128,256]{3,2,1,0:T(8,128)} copy(f32[2,4,128,256]{2,3,1,0:T(8,128)S(1)} %bitcast.16) | data formatting | bytes 2097152
where the time goes:
time: 125 us; the launch traced here: 124 us
  Pallas kernels  116 us (93%)
  local copies, waits for them, and re-layouts  7.99 us (6%)
    pallas_call x1, Pallas kernels, per_device(): pl.pallas_call(functools.partial(solve_kernel, peers, spaces, chunks, mod...  116 us
    unnamed x3, local copies, waits for them, and re-layouts  4.18 us
    reshape x2, local copies, waits for them, and re-layouts, back(): value = value.reshape(peers, chunks, layers, lc, face, blk)  2.7 us

commit v1 on v0

v1 whole, which is shorter than its diff:
```python
import functools

import jax
import jax.numpy as jnp
from jax import lax
from jax.experimental import pallas as pl
from jax.experimental.pallas import tpu as pltpu
from jax.sharding import PartitionSpec as P

DEGREE = 4
COUPLING = 0.5773502691896258
THETA = 1.0
DELTA = 0.7
CHUNKS = 4
GROUP = 2
LAG = 4
LEAD = 3
SLOTS = 4
RELAYED_GROUP = 1
VMEM_LIMIT = 56_000_000
MESH = pl.DeviceIdType.MESH


def prepare(raw, e, slot, modes_dev, adj_ref, mask_ref, w_hi, w_lo):
    face, blk = w_hi.shape[1], raw.shape[2]
    layer, f = e // face, lax.rem(e, face)
    for op in range(w_hi.shape[3] // blk):
        if op == 0:
            weights = [None]
        else:
            weights = [
                jnp.where(mask_ref[j] == modes_dev * (1 << (op - 1)), COUPLING, 0.0).astype(jnp.float32)
                for j in range(raw.shape[1] - 1)
            ]

        def block(s):
            lanes = slice(s * blk, (s + 1) * blk)
            if op == 0:
                return raw[slot, 0, :, lanes]
            total = weights[0] * raw[slot, 1, :, lanes]
            for j in range(1, len(weights)):
                total = total + weights[j] * raw[slot, 1 + j, :, lanes]
            return total

        own = block(0)
        sides = [block(3 + s) for s in range(adj_ref.shape[2])]
        parts = []
        for g in range(face):
            total = jnp.where(f == g, 1.0, 0.0).astype(jnp.float32) * own
            for s, side in enumerate(sides):
                total = total + jnp.where(adj_ref[layer, f, s] == g, 1.0, 0.0).astype(jnp.float32) * side
            parts.append(total)
        parts += [block(1), block(2)]
        for at, part in enumerate(parts):
            part = part.T
            high = part.astype(jnp.bfloat16)
            low = (part - high.astype(jnp.float32)).astype(jnp.bfloat16)
            w_hi[layer, f, at * blk : (at + 1) * blk, op * blk : (op + 1) * blk] = high
            w_lo[layer, f, at * blk : (at + 1) * blk, op * blk : (op + 1) * blk] = low


def schedule(chunks):
    steps = []
    group = min(GROUP, chunks)
    for turn in range(DEGREE + LAG * (chunks // group - 1)):
        for place in range(group):
            for c in range(place, chunks, group):
                t = turn - LAG * (c // group)
                if 0 <= t < DEGREE:
                    steps.append((t, c))
    items = []
    for at, step in enumerate(steps):
        for c in range(chunks):
            if max(steps.index((0, c)) - (LEAD if c >= group else 0), 0) == at:
                items.append((-1, c))
        items.append(step)
    plan = []
    for at, item in enumerate(items):
        ahead = items[at + 1] if at + 1 < len(items) else (-1, 0)
        if ahead[0] < 0 and at + 2 < len(items) and item[0] < 0:
            ahead = items[at + 2]
        if any(ahead == done[2:] for done in plan) or ahead[0] < 0:
            ahead = (-1, 0)
        plan.append(item + ahead)
    missing = [item for item in items if item[0] >= 0 and item not in [done[2:] for done in plan]]
    assert not missing, missing
    return plan


def solve_kernel(
    peers, spaces, chunks, modes_dev, source, mean, fields, adj, masks, x_out, r_out,
    raw, w_hi, w_lo, direction, res, x, split, acc, halo_low, halo_up, relay, stage, src, x_land, r_land,
    w_sem, stage_sem, own_sem, in_send, in_recv, low_send, low_recv, up_send, up_recv,
    relay_send, relay_recv, forward_send, forward_recv, out_send, out_recv, own_out,
):
    layers, face, inner, width = w_hi.shape
    blk = inner // (face + 2)
    bits = peers.bit_length() - 1
    rows = direction.shape[4]
    lc = rows // peers
    me = lax.axis_index("mode")
    s = lax.axis_index("space")
    has_low = s > 0
    has_up = s < spaces - 1
    relayed = spaces >= 4 and spaces % 2 == 0 and face % 2 == 0
    groups = 2 if face % 2 == 0 else 1
    per = face // groups
    odd = lax.rem(s, 2) == 1
    even = jnp.logical_not(odd)
    both = jnp.logical_and
    elements = layers * face

    def loads(e):
        slot = lax.rem(e, SLOTS)
        l, f = e // face, lax.rem(e, face)
        return (
            pltpu.make_async_copy(mean.at[l, f], raw.at[slot, 0], w_sem.at[slot, 0]),
            pltpu.make_async_copy(fields.at[:, l, f], raw.at[slot, pl.ds(1, fields.shape[0])], w_sem.at[slot, 1]),
        )

    fetch = pltpu.make_async_copy(source, stage, stage_sem.at[0])
    fetch.start()
    for e in range(min(SLOTS, elements)):
        for load in loads(e):
            load.start()

    barrier = pltpu.get_barrier_semaphore()
    for k in range(1, peers):
        pl.semaphore_signal(barrier, inc=1, device_id={"mode": lax.rem(me + k, peers)}, device_id_type=MESH)

    @pl.when(has_low)
    def _():
        pl.semaphore_signal(barrier, inc=1, device_id={"space": s - 1}, device_id_type=MESH)

    @pl.when(has_up)
    def _():
        pl.semaphore_signal(barrier, inc=1, device_id={"space": s + 1}, device_id_type=MESH)

    expected = peers - 1 + has_low.astype(jnp.int32) + has_up.astype(jnp.int32)
    if relayed:
        far_low, far_up = s >= 2, s < spaces - 2
        expected = expected + far_low.astype(jnp.int32) + far_up.astype(jnp.int32)

        @pl.when(far_low)
        def _():
            pl.semaphore_signal(barrier, inc=1, device_id={"space": s - 2}, device_id_type=MESH)

        @pl.when(far_up)
        def _():
            pl.semaphore_signal(barrier, inc=1, device_id={"space": s + 2}, device_id_type=MESH)

    bands = min(chunks, max(modes_dev // 128, 1))
    band = modes_dev // bands
    in_band = chunks // bands
    fetch.wait()
    for n in range(bands):
        modes = slice(n * band, (n + 1) * band)
        for l in range(layers):
            for f in range(face):
                src[l, f, modes] = stage[l, f, :, modes].T * (1.0 / THETA)

    with jax.named_scope('barrier'):
        pl.semaphore_wait(barrier, expected)

    def slab(ref, c, h):
        return ref.at[c, :, :, pl.ds(pl.multiple_of(h * lc, lc), lc), :]

    def piece(ref, c, h):
        return ref.at[:, :, pl.ds(pl.multiple_of((c * peers + h) * lc, lc), lc), :]

    def in_copy(c, k):
        to = lax.rem(me + k, peers)
        return pltpu.make_async_remote_copy(
            src_ref=piece(src, c, to), dst_ref=slab(direction.at[0], c, me),
            send_sem=in_send.at[0], recv_sem=in_recv.at[c],
            device_id={"mode": to}, device_id_type=MESH,
        )

    def whole(ref, count, send_sem, recv_sem):
        part = ref.at[:, :, pl.ds(0, count), :]
        return pltpu.make_async_remote_copy(
            src_ref=part, dst_ref=part, send_sem=send_sem, recv_sem=recv_sem,
            device_id={"mode": lax.rem(me + 1, peers)}, device_id_type=MESH,
        )

    def own_copy(c):
        return pltpu.make_async_copy(piece(src, c, me), slab(direction.at[0], c, me), own_sem.at[c])

    def to_low(t, c, g):
        part = pl.ds(g * per, per)
        return pltpu.make_async_remote_copy(
            src_ref=direction.at[lax.rem(t, 2), c, 0, part], dst_ref=halo_up.at[t, c, part],
            send_sem=low_send.at[lax.rem(t, 2), c, g], recv_sem=up_recv.at[lax.rem(t, 2), c, g],
            device_id={"space": s - 1}, device_id_type=MESH,
        )

    def to_up(t, c, g):
        part = pl.ds(g * per, per)
        return pltpu.make_async_remote_copy(
            src_ref=direction.at[lax.rem(t, 2), c, layers - 1, part], dst_ref=halo_low.at[t, c, part],
            send_sem=up_send.at[lax.rem(t, 2), c, g], recv_sem=low_recv.at[lax.rem(t, 2), c, g],
            device_id={"space": s + 1}, device_id_type=MESH,
        )

    def to_relay(t, c, layer, offset):
        return pltpu.make_async_remote_copy(
            src_ref=direction.at[lax.rem(t, 2), c, layer, pl.ds(RELAYED_GROUP * per, per)], dst_ref=relay.at[t, c],
            send_sem=relay_send.at[lax.rem(t, 2), c], recv_sem=relay_recv.at[lax.rem(t, 2), c],
            device_id={"space": s + offset}, device_id_type=MESH,
        )

    def forward(t, c, halo, offset):
        return pltpu.make_async_remote_copy(
            src_ref=relay.at[t, c], dst_ref=halo.at[t, c, pl.ds(RELAYED_GROUP * per, per)],
            send_sem=forward_send.at[0], recv_sem=forward_recv.at[lax.rem(t, 2), c],
            device_id={"space": s + offset}, device_id_type=MESH,
        )

    def halo_each(t, c, g, act):
        hop = relayed and g == RELAYED_GROUP

        @pl.when(both(even, has_low))
        def _():
            act(to_relay(t, c, 0, -2) if hop else to_low(t, c, g))

        @pl.when(both(odd, has_up))
        def _():
            act(to_relay(t, c, layers - 1, 2) if hop else to_up(t, c, g))

        @pl.when(both(odd, has_low))
        def _():
            act(to_low(t, c, g))

        @pl.when(both(even, has_up))
        def _():
            act(to_up(t, c, g))

    def halo_start(t, c, g):
        halo_each(t, c, g, lambda copy: copy.start())

    def halo_sent(t, c):
        for g in range(groups):
            halo_each(t, c, g, lambda copy: copy.wait_send())

    def forward_each(t, c, act):
        if relayed:

            @pl.when(both(odd, s >= 3))
            def _():
                act(forward(t, c, halo_low, -1))

            @pl.when(both(even, s < spaces - 3))
            def _():
                act(forward(t, c, halo_up, 1))

    def halo_forward(t, c):
        if relayed:

            @pl.when(jnp.logical_or(both(odd, s >= 3), both(even, s < spaces - 3)))
            def _():
                to_relay(t, c, 0, jnp.where(odd, -1, 1)).wait_recv()

            forward_each(t, c, lambda copy: copy.start())

    def halo_arrived(t, c, g):
        hop = relayed and g == RELAYED_GROUP

        @pl.when(both(odd, has_low))
        def _():
            to_up(t, c, g).wait_recv()

        @pl.when(both(even, has_up))
        def _():
            to_low(t, c, g).wait_recv()

        @pl.when(both(even, has_low))
        def _():
            (forward(t, c, halo_low, -1) if hop else to_up(t, c, g)).wait_recv()

        @pl.when(both(odd, has_up))
        def _():
            (forward(t, c, halo_up, 1) if hop else to_low(t, c, g)).wait_recv()

    def out_start(which, ref, land, c):
        for k in range(1, peers):
            to = lax.rem(me + k, peers)
            pltpu.make_async_remote_copy(
                src_ref=slab(ref, c, to), dst_ref=piece(land, c, me),
                send_sem=out_send.at[which], recv_sem=out_recv.at[which, c // in_band],
                device_id={"mode": to}, device_id_type=MESH,
            ).start()
        pltpu.make_async_copy(slab(ref, c, me), piece(land, c, me), own_out.at[which, c // in_band]).start()

    def out_finish(which, land, out, n):
        count = in_band * (peers - 1) * lc
        whole(land, count, out_send.at[which], out_recv.at[which, n]).wait_recv()
        own = land.at[:, :, pl.ds(0, in_band * lc), :]
        pltpu.make_async_copy(own, own, own_out.at[which, n]).wait()
        modes = slice(n * band, (n + 1) * band)
        for l in range(layers):
            for f in range(face):
                out[l, f, :, modes] = land[l, f, modes].T

    for c in range(chunks):
        for k in range(1, peers):
            in_copy(c, k).start()
        own_copy(c).start()

    @pl.when(jnp.logical_not(has_low))
    def _():
        halo_low[...] = jnp.zeros_like(halo_low)

    @pl.when(jnp.logical_not(has_up))
    def _():
        halo_up[...] = jnp.zeros_like(halo_up)

    def land(c):
        own_copy(c).wait()
        whole(src, (peers - 1) * lc, in_send.at[0], in_recv.at[c]).wait_recv()
        for g in range(groups):
            halo_start(0, c, g)

    items = schedule(chunks)

    def build(e, carry):
        for load in loads(e):
            load.wait()
        prepare(raw, e, lax.rem(e, SLOTS), modes_dev, adj, masks, w_hi, w_lo)

        @pl.when(e + SLOTS < elements)
        def _():
            for load in loads(e + SLOTS):
                load.start()

        return carry

    with jax.named_scope('build'):
        lax.fori_loop(0, elements, build, 0)

    def halves(value):
        high = value.astype(jnp.bfloat16)
        return high, (value - high.astype(jnp.float32)).astype(jnp.bfloat16)

    def product(a, l, f, lo, hi):
        def dot(left, right):
            return lax.dot_general(left, right, (((1,), (0,)), ((), ())), preferred_element_type=jnp.float32)

        y = dot(a, w_hi[l, f, lo:hi])
        return y[:rows] + y[rows:] + dot(a[:rows], w_lo[l, f, lo:hi])

    def keep_split(c, l, f, value):
        high, low = halves(value)
        split[c, l, :rows, f * blk : (f + 1) * blk] = high
        split[c, l, rows:, f * blk : (f + 1) * blk] = low

    sigma = THETA / DELTA
    last = (DEGREE - 1) % 2
    ratios = [1.0 / sigma]
    for _ in range(DEGREE):
        ratios.append(1.0 / (2.0 * sigma - ratios[-1]))

    def item(i):
        found = [jnp.int32(-1)] * 4
        for at, entry in enumerate(items):
            found = [jnp.where(i == at, value, old) for value, old in zip(entry, found)]
        return found

    def side(c, l, f, halo, t):
        if 0 <= l < layers:
            return split[c, l, :, f * blk : (f + 1) * blk]
        return jnp.concatenate(halves(halo[t, c, f]), axis=0)

    def advance(i, carry):
        t, c, t_next, c_next = item(i)

        @pl.when(t < 0)
        def _():
            with jax.named_scope('land'):
                land(c)

            for l in range(layers):
                for f in range(face):
                    d = direction[0, c, l, f]
                    res[c, l, f] = d
                    x[0, c, l, f] = d
                    keep_split(c, l, f, d)

        now = lax.rem(t + 2, 2)
        keep, add = jnp.float32(0.0), jnp.float32(0.0)
        for at in range(DEGREE - 1):
            keep = jnp.where(t == at, jnp.float32(ratios[at + 1] * ratios[at]), keep)
            add = jnp.where(t == at, jnp.float32(2.0 * ratios[at + 1] / DELTA), add)

        for g in range(groups):

            @pl.when(t >= 0)
            def _():
                with jax.named_scope(f'wait{g}'):
                    halo_arrived(t, c, g)

                if g == 0:

                    @pl.when(t > 0)
                    def _():
                        halo_sent(t - 1, c)

                for f in range(g * per, (g + 1) * per):
                    ys = []
                    for l in range(layers):
                        a = jnp.concatenate([side(c, l - 1, f, halo_low, t), side(c, l + 1, f, halo_up, t)], axis=1)
                        ys.append(acc[c, l, f] + product(a, l, f, face * blk, inner))
                    for l, y in enumerate(ys):
                        d = direction[now, c, l, f]
                        total = d + y[:, :blk]
                        for b in range(bits):
                            term = y[:, (b + 1) * blk : (b + 2) * blk]
                            total = total + jnp.concatenate(
                                [term[(h ^ (1 << b)) * lc : ((h ^ (1 << b)) + 1) * lc] for h in range(peers)], axis=0
                            )
                        r = res[c, l, f] - total
                        res[c, l, f] = r
                        d_new = keep * d + add * r
                        direction[1 - now, c, l, f] = d_new
                        x[1 - now, c, l, f] = x[now, c, l, f] + d_new
                        keep_split(c, l, f, d_new)

                @pl.when(t < DEGREE - 1)
                def _():
                    halo_start(t + 1, c, g)

        @pl.when(t == DEGREE - 2)
        def _():
            out_start(0, x.at[last], x_land, c)

        @pl.when(t == DEGREE - 1)
        def _():
            out_start(1, res, r_land, c)

        @pl.when(t < DEGREE - 1)
        def _():
            for l in range(layers):
                a = split[c, l]
                for f in range(face):
                    acc[c, l, f] = product(a, l, f, 0, face * blk)

        @pl.when(t_next >= 0)
        def _():
            with jax.named_scope('fwd'):
                halo_forward(t_next, c_next)

        return carry

    lax.fori_loop(0, len(items), advance, 0)

    with jax.named_scope('sent'):
        for c in range(chunks):
            halo_sent(DEGREE - 1, c)
        everything = (peers - 1) * chunks * lc
        whole(src, everything, in_send.at[0], in_recv.at[0]).wait_send()
        if relayed:

            @pl.when(jnp.logical_or(both(odd, s >= 3), both(even, s < spaces - 3)))
            def _():
                pltpu.make_async_remote_copy(
                    src_ref=relay, dst_ref=relay, send_sem=forward_send.at[0], recv_sem=forward_recv.at[0, 0],
                    device_id={"space": s + jnp.where(odd, -1, 1)}, device_id_type=MESH,
                ).wait_send()

    for n in range(bands):
        with jax.named_scope(f'finx{n}'):
            out_finish(0, x_land, x_out, n)
        with jax.named_scope(f'finr{n}'):
            out_finish(1, r_land, r_out, n)
    with jax.named_scope('end'):
        for which, land, out in ((0, x_land, x_out), (1, r_land, r_out)):
            whole(land, everything, out_send.at[which], out_recv.at[which, 0]).wait_send()


def deliver(x, r, x_out, r_out, sem):
    copies = [pltpu.make_async_copy(x, x_out, sem.at[0]), pltpu.make_async_copy(r, r_out, sem.at[1])]
    for copy in copies:
        copy.start()
    for copy in copies:
        copy.wait()


def per_device(peers, spaces, source_field, mean_operator, field_operators, adjacency, mode_masks):
    layers, face, blk, modes_dev = source_field.shape
    bits = peers.bit_length() - 1
    chunks = CHUNKS
    while modes_dev % (peers * chunks * 8):
        chunks //= 2
    rows = modes_dev // chunks
    groups = 2 if face % 2 == 0 else 1
    weights = pltpu.VMEM((layers, face, (face + 2) * blk, (bits + 1) * blk), jnp.bfloat16)
    out = pltpu.VMEM(source_field.shape, jnp.float32)
    landing = pltpu.VMEM((layers, face, modes_dev, blk), jnp.float32)
    bands = min(chunks, max(modes_dev // 128, 1))
    field = (chunks, layers, face, rows, blk)
    halo = pltpu.VMEM((DEGREE, chunks, face, rows, blk), jnp.float32)
    dma = pltpu.SemaphoreType.DMA
    x, r = pl.pallas_call(
        functools.partial(solve_kernel, peers, spaces, chunks, modes_dev),
        in_specs=[
            pl.BlockSpec(memory_space=pl.ANY),
            pl.BlockSpec(memory_space=pl.ANY),
            pl.BlockSpec(memory_space=pl.ANY),
            pl.BlockSpec(memory_space=pltpu.SMEM),
            pl.BlockSpec(memory_space=pltpu.SMEM),
        ],
        out_specs=(pl.BlockSpec(memory_space=pltpu.VMEM), pl.BlockSpec(memory_space=pltpu.VMEM)),
        out_shape=(out, out),
        scratch_shapes=[
            pltpu.VMEM((SLOTS, 1 + field_operators.shape[0]) + mean_operator.shape[2:], jnp.float32),
            weights,
            weights,
            pltpu.VMEM((2,) + field, jnp.float32),
            pltpu.VMEM(field, jnp.float32),
            pltpu.VMEM((2,) + field, jnp.float32),
            pltpu.VMEM((chunks, layers, 2 * rows, face * blk), jnp.bfloat16),
            pltpu.VMEM((chunks, layers, face, rows, (bits + 1) * blk), jnp.float32),
            halo,
            halo,
            pltpu.VMEM((DEGREE, chunks, face // groups, rows, blk), jnp.float32),
            pltpu.VMEM(source_field.shape, jnp.float32),
            landing,
            landing,
            landing,
            dma((SLOTS, 2)),
            dma((1,)),
            dma((chunks,)),
            dma((1,)),
            dma((chunks,)),
            dma((2, chunks, groups)),
            dma((2, chunks, groups)),
            dma((2, chunks, groups)),
            dma((2, chunks, groups)),
            dma((2, chunks)),
            dma((2, chunks)),
            dma((1,)),
            dma((2, chunks)),
            dma((2,)),
            dma((2, bands)),
            dma((2, bands)),
        ],
        compiler_params=pltpu.CompilerParams(
            collective_id=0, has_side_effects=True, vmem_limit_bytes=VMEM_LIMIT
        ),
    )(source_field, mean_operator, field_operators, adjacency, mode_masks)
    return x, r


def solution(mesh):
    in_specs = (
        P("space", None, None, "mode"),
        P("space", None, None, None),
        P(None, "space", None, None, None),
        P("space", None, None),
        P(),
    )
    out_specs = (P("space", None, None, "mode"), P("space", None, None, "mode"))
    return jax.shard_map(
        functools.partial(per_device, mesh.shape["mode"], mesh.shape["space"]),
        mesh=mesh, in_specs=in_specs, out_specs=out_specs, check_vma=False,
    )
```

time: 125 us -> 105 us (0.84)
  Pallas kernels: 116 us -> 102 us
  local copies, waits for them, and re-layouts: 7.99 us -> 1.94 us
    pallas_call x1, Pallas kernels: 116 us -> 102 us  [per_device(): pl.pallas_call(functools.partial(solve_kernel, peers, spaces, chunks, mod...]
    reshape x2 -> x0, local copies, waits for them, and re-layouts: 2.7 us -> none  [back(): value = value.reshape(peers, chunks, layers, lc, face, blk)]
    unnamed x3 -> x2, local copies, waits for them, and re-layouts: 4.18 us -> 1.94 us
where the time goes in v1:
time: 105 us; the launch traced here: 104 us
  Pallas kernels  102 us (97%)
  local copies, waits for them, and re-layouts  1.94 us (2%)
    pallas_call x1, Pallas kernels, per_device(): pl.pallas_call(functools.partial(solve_kernel, peers, spaces, chunks, mod...  102 us

profile of v1, /device:TPU:5, one launch (start us, length us, event | category | flops | bytes accessed | tf_op | source)
XLA Modules:
  0.0 104.3 jit_solution(4599131664342919599)
XLA Ops:
  0.6 101.7 %shard_map.68 = (f32[2,4,128,256]{3,2,1,0:T(8,128)S(1)}, f32[2,4,128,256]{3,2,1,0:T(8,128)S(1)}) custom-call(f32[2,4,128,256]{3,2,1,0:T(8,128)} %source.1, f32[2,4,128,896]{3,2,1,0:T(8,128)} %mean.1, f32[4,2,4,128,896]{4,3,2,1,0:T(8,128)} %fields.1, s32[2,4,4]{2,1,0:T(4,128)} %adj.1, s32[4]{0:T(128)} %masks.1), custom_call_target="tpu_custom_call" | custom-call | tf_op jit(solution)/shard_map/pallas_call | solution.py:502
  102.4 1.0 copy.9
  103.3 1.0 copy.10

commit v2 on v1

--- a/solution.py
+++ b/solution.py
@@ -16,6 +16,8 @@
 LAG = 4
 LEAD = 3
 SLOTS = 4
+SECOND = 5
+ORDER = ((-1, 0), (-1, 1), (0, 0), (0, 1), (1, 0), (1, 1), (2, 0), (-1, 2), (2, 1), (0, 2), (3, 0), (-1, 3), (1, 2), (3, 1), (0, 3), (2, 2), (1, 3), (3, 2), (2, 3), (3, 3))
 RELAYED_GROUP = 1
 VMEM_LIMIT = 56_000_000
 MESH = pl.DeviceIdType.MESH
@@ -60,30 +62,24 @@
 
 
 def schedule(chunks):
-    steps = []
     group = min(GROUP, chunks)
-    for turn in range(DEGREE + LAG * (chunks // group - 1)):
-        for place in range(group):
-            for c in range(place, chunks, group):
+    items = list(ORDER) if chunks == CHUNKS else []
+    if not items:
+        items = [(-1, c) for c in range(chunks)]
+        for turn in range(DEGREE + LAG * (chunks // group - 1)):
+            for c in range(chunks):
                 t = turn - LAG * (c // group)
                 if 0 <= t < DEGREE:
-                    steps.append((t, c))
-    items = []
-    for at, step in enumerate(steps):
-        for c in range(chunks):
-            if max(steps.index((0, c)) - (LEAD if c >= group else 0), 0) == at:
-                items.append((-1, c))
-        items.append(step)
-    plan = []
+                    items.append((t, c))
+    assert sorted(items) == [(t, c) for t in range(-1, DEGREE) for c in range(chunks)]
+    plan, told = [], set()
     for at, item in enumerate(items):
-        ahead = items[at + 1] if at + 1 < len(items) else (-1, 0)
-        if ahead[0] < 0 and at + 2 < len(items) and item[0] < 0:
-            ahead = items[at + 2]
-        if any(ahead == done[2:] for done in plan) or ahead[0] < 0:
-            ahead = (-1, 0)
-        plan.append(item + ahead)
-    missing = [item for item in items if item[0] >= 0 and item not in [done[2:] for done in plan]]
-    assert not missing, missing
+        ahead = [step for step in items[at + 1 :] if step[0] >= 0][:1]
+        if ahead and (ahead[0] in told or (ahead[0][0] - 1, ahead[0][1]) not in items[: at + 1]):
+            ahead = []
+        plan.append(item + (ahead[0] if ahead else (-1, 0)))
+        told.update(ahead)
+    assert told == {item for item in items if item[0] >= 0}
     return plan
 
 
@@ -118,8 +114,23 @@
             pltpu.make_async_copy(fields.at[:, l, f], raw.at[slot, pl.ds(1, fields.shape[0])], w_sem.at[slot, 1]),
         )
 
-    fetch = pltpu.make_async_copy(source, stage, stage_sem.at[0])
-    fetch.start()
+    bands = min(chunks, max(modes_dev // 128, 1))
+    band = modes_dev // bands
+    in_band = chunks // bands
+
+    def fetch(n):
+        modes = pl.ds(n * band, band)
+        return pltpu.make_async_copy(source.at[:, :, :, modes], stage.at[:, :, :, modes], stage_sem.at[n])
+
+    def turn(n):
+        fetch(n).wait()
+        modes = slice(n * band, (n + 1) * band)
+        for l in range(layers):
+            for f in range(face):
+                src[l, f, modes] = stage[l, f, :, modes].T * (1.0 / THETA)
+
+    for n in range(bands):
+        fetch(n).start()
     for e in range(min(SLOTS, elements)):
         for load in loads(e):
             load.start()
@@ -149,35 +160,32 @@
         def _():
             pl.semaphore_signal(barrier, inc=1, device_id={"space": s + 2}, device_id_type=MESH)
 
-    bands = min(chunks, max(modes_dev // 128, 1))
-    band = modes_dev // bands
-    in_band = chunks // bands
-    fetch.wait()
-    for n in range(bands):
-        modes = slice(n * band, (n + 1) * band)
-        for l in range(layers):
-            for f in range(face):
-                src[l, f, modes] = stage[l, f, :, modes].T * (1.0 / THETA)
-
+    turn(0)
     with jax.named_scope('barrier'):
         pl.semaphore_wait(barrier, expected)
 
-    def slab(ref, c, h):
-        return ref.at[c, :, :, pl.ds(pl.multiple_of(h * lc, lc), lc), :]
-
-    def piece(ref, c, h):
-        return ref.at[:, :, pl.ds(pl.multiple_of((c * peers + h) * lc, lc), lc), :]
-
-    def in_copy(c, k):
-        to = lax.rem(me + k, peers)
-        return pltpu.make_async_remote_copy(
-            src_ref=piece(src, c, to), dst_ref=slab(direction.at[0], c, me),
-            send_sem=in_send.at[0], recv_sem=in_recv.at[c],
-            device_id={"mode": to}, device_id_type=MESH,
-        )
-
-    def whole(ref, count, send_sem, recv_sem):
-        part = ref.at[:, :, pl.ds(0, count), :]
+    def slab(ref, c, h, part=slice(None)):
+        return ref.at[c, :, part, pl.ds(pl.multiple_of(h * lc, lc), lc), :]
+
+    def piece(ref, c, h, part=slice(None)):
+        return ref.at[:, part, pl.ds(pl.multiple_of((c * peers + h) * lc, lc), lc), :]
+
+    hops = sorted(range(1, peers), key=lambda k: abs(k - peers // 2))
+
+    def in_start(c):
+        for g in reversed(range(groups)) if RELAYED_GROUP else range(groups):
+            part = pl.ds(g * per, per)
+            for k in hops:
+                to = lax.rem(me + k, peers)
+                pltpu.make_async_remote_copy(
+                    src_ref=piece(src, c, to, part), dst_ref=slab(direction.at[0], c, me, part),
+                    send_sem=in_send.at[0], recv_sem=in_recv.at[c, g],
+                    device_id={"mode": to}, device_id_type=MESH,
+                ).start()
+        own_copy(c).start()
+
+    def whole(ref, count, send_sem, recv_sem, faces=face):
+        part = ref.at[:, pl.ds(0, faces), pl.ds(0, count), :]
         return pltpu.make_async_remote_copy(
             src_ref=part, dst_ref=part, send_sem=send_sem, recv_sem=recv_sem,
             device_id={"mode": lax.rem(me + 1, peers)}, device_id_type=MESH,
@@ -282,7 +290,7 @@
             (forward(t, c, halo_up, 1) if hop else to_low(t, c, g)).wait_recv()
 
     def out_start(which, ref, land, c):
-        for k in range(1, peers):
+        for k in hops:
             to = lax.rem(me + k, peers)
             pltpu.make_async_remote_copy(
                 src_ref=slab(ref, c, to), dst_ref=piece(land, c, me),
@@ -301,10 +309,9 @@
             for f in range(face):
                 out[l, f, :, modes] = land[l, f, modes].T
 
-    for c in range(chunks):
-        for k in range(1, peers):
-            in_copy(c, k).start()
-        own_copy(c).start()
+    in_start(0)
+    for n in range(1, bands):
+        turn(n)
 
     @pl.when(jnp.logical_not(has_low))
     def _():
@@ -316,9 +323,14 @@
 
     def land(c):
         own_copy(c).wait()
-        whole(src, (peers - 1) * lc, in_send.at[0], in_recv.at[c]).wait_recv()
-        for g in range(groups):
+        for g in reversed(range(groups)) if RELAYED_GROUP else range(groups):
+            whole(src, (peers - 1) * lc, in_send.at[0], in_recv.at[c, g], per).wait_recv()
             halo_start(0, c, g)
+
+        @pl.when(c == min(1, chunks - 1))
+        def _():
+            for late in range(2, chunks):
+                in_start(late)
 
     items = schedule(chunks)
 
@@ -331,6 +343,12 @@
         def _():
             for load in loads(e + SLOTS):
                 load.start()
+
+        if chunks > 1:
+
+            @pl.when(e == SECOND)
+            def _():
+                in_start(1)
 
         return carry
 
@@ -456,7 +474,7 @@
         for c in range(chunks):
             halo_sent(DEGREE - 1, c)
         everything = (peers - 1) * chunks * lc
-        whole(src, everything, in_send.at[0], in_recv.at[0]).wait_send()
+        whole(src, everything, in_send.at[0], in_recv.at[0, 0]).wait_send()
         if relayed:
 
             @pl.when(jnp.logical_or(both(odd, s >= 3), both(even, s < spaces - 3)))
@@ -527,10 +545,10 @@
             landing,
             landing,
             dma((SLOTS, 2)),
-            dma((1,)),
+            dma((bands,)),
             dma((chunks,)),
             dma((1,)),
-            dma((chunks,)),
+            dma((chunks, groups)),
             dma((2, chunks, groups)),
             dma((2, chunks, groups)),
             dma((2, chunks, groups)),

time: 105 us -> 99.5 us (0.948)
  Pallas kernels: 102 us -> 95.7 us
    pallas_call x1, Pallas kernels: 102 us -> 95.7 us  [per_device(): pl.pallas_call(functools.partial(solve_kernel, peers, spaces, chunks, mod...]
where the time goes in v2:
time: 99.5 us; the launch traced here: 98.3 us
  Pallas kernels  95.7 us (96%)
  local copies, waits for them, and re-layouts  1.94 us (2%)
    pallas_call x1, Pallas kernels, per_device(): pl.pallas_call(functools.partial(solve_kernel, peers, spaces, chunks, mod...  95.7 us

profile of v2, /device:TPU:5, one launch (start us, length us, event | category | flops | bytes accessed | tf_op | source)
XLA Modules:
  0.0 98.3 jit_solution(5027049556274842800)
XLA Ops:
  0.6 95.7 %shard_map.68 = (f32[2,4,128,256]{3,2,1,0:T(8,128)S(1)}, f32[2,4,128,256]{3,2,1,0:T(8,128)S(1)}) custom-call(f32[2,4,128,256]{3,2,1,0:T(8,128)} %source.1, f32[2,4,128,896]{3,2,1,0:T(8,128)} %mean.1, f32[4,2,4,128,896]{4,3,2,1,0:T(8,128)} %fields.1, s32[2,4,4]{2,1,0:T(4,128)} %adj.1, s32[4]{0:T(128)} %masks.1), custom_call_target="tpu_custom_call" | custom-call | tf_op jit(solution)/shard_map/pallas_call | solution.py:520
  96.3 1.0 copy.9
  97.3 1.0 copy.10

commit v3 on v2

--- a/solution.py
+++ b/solution.py
@@ -17,7 +17,8 @@
 LEAD = 3
 SLOTS = 4
 SECOND = 5
-ORDER = ((-1, 0), (-1, 1), (0, 0), (0, 1), (1, 0), (1, 1), (2, 0), (-1, 2), (2, 1), (0, 2), (3, 0), (-1, 3), (1, 2), (3, 1), (0, 3), (2, 2), (1, 3), (3, 2), (2, 3), (3, 3))
+EARLY = 0
+ORDER = ((-1, 0), (-1, 1), (0, 0), (0, 1), (1, 0), (-1, 2), (1, 1), (2, 0), (0, 2), (2, 1), (3, 0), (-1, 3), (1, 2), (3, 1), (0, 3), (2, 2), (1, 3), (3, 2), (2, 3), (3, 3))
 RELAYED_GROUP = 1
 VMEM_LIMIT = 56_000_000
 MESH = pl.DeviceIdType.MESH
@@ -123,7 +124,8 @@
         return pltpu.make_async_copy(source.at[:, :, :, modes], stage.at[:, :, :, modes], stage_sem.at[n])
 
     def turn(n):
-        fetch(n).wait()
+        with jax.named_scope('fetch'):
+            fetch(n).wait()
         modes = slice(n * band, (n + 1) * band)
         for l in range(layers):
             for f in range(face):
@@ -131,9 +133,6 @@
 
     for n in range(bands):
         fetch(n).start()
-    for e in range(min(SLOTS, elements)):
-        for load in loads(e):
-            load.start()
 
     barrier = pltpu.get_barrier_semaphore()
     for k in range(1, peers):
@@ -161,6 +160,9 @@
             pl.semaphore_signal(barrier, inc=1, device_id={"space": s + 2}, device_id_type=MESH)
 
     turn(0)
+    for e in range(min(SLOTS, elements)):
+        for load in loads(e):
+            load.start()
     with jax.named_scope('barrier'):
         pl.semaphore_wait(barrier, expected)
 
@@ -321,16 +323,11 @@
     def _():
         halo_up[...] = jnp.zeros_like(halo_up)
 
-    def land(c):
-        own_copy(c).wait()
-        for g in reversed(range(groups)) if RELAYED_GROUP else range(groups):
-            whole(src, (peers - 1) * lc, in_send.at[0], in_recv.at[c, g], per).wait_recv()
-            halo_start(0, c, g)
-
-        @pl.when(c == min(1, chunks - 1))
-        def _():
-            for late in range(2, chunks):
-                in_start(late)
+    turns = list(reversed(range(groups))) if RELAYED_GROUP else list(range(groups))
+
+    def land(c, g):
+        whole(src, (peers - 1) * lc, in_send.at[0], in_recv.at[c, g], per).wait_recv()
+        halo_start(0, c, g)
 
     items = schedule(chunks)
 
@@ -349,6 +346,14 @@
             @pl.when(e == SECOND)
             def _():
                 in_start(1)
+
+        for place, g in enumerate(turns):
+
+            @pl.when(e == elements - groups + place - EARLY)
+            def _():
+                if place == 0:
+                    own_copy(0).wait()
+                land(0, g)
 
         return carry
 
@@ -393,8 +398,17 @@
 
         @pl.when(t < 0)
         def _():
-            with jax.named_scope('land'):
-                land(c)
+            @pl.when(c > 0)
+            def _():
+                with jax.named_scope('land'):
+                    own_copy(c).wait()
+                    for g in turns:
+                        land(c, g)
+
+            @pl.when(c == min(1, chunks - 1))
+            def _():
+                for late in range(2, chunks):
+                    in_start(late)
 
             for l in range(layers):
                 for f in range(face):

time: 99.5 us -> 98.7 us (level); the launches traced: 98.3 us -> 98.5 us
  no operation moved by 1% of the time
where the time goes in v3:
time: 98.7 us; the launch traced here: 98.5 us
  Pallas kernels  96 us (97%)
  local copies, waits for them, and re-layouts  1.94 us (2%)
    pallas_call x1, Pallas kernels, per_device(): pl.pallas_call(functools.partial(solve_kernel, peers, spaces, chunks, mod...  96 us

profile of v3, /device:TPU:5, one launch (start us, length us, event | category | flops | bytes accessed | tf_op | source)
XLA Modules:
  0.0 98.5 jit_solution(17519911573234300042)
XLA Ops:
  0.6 96.0 %shard_map.68 = (f32[2,4,128,256]{3,2,1,0:T(8,128)S(1)}, f32[2,4,128,256]{3,2,1,0:T(8,128)S(1)}) custom-call(f32[2,4,128,256]{3,2,1,0:T(8,128)} %source.1, f32[2,4,128,896]{3,2,1,0:T(8,128)} %mean.1, f32[4,2,4,128,896]{4,3,2,1,0:T(8,128)} %fields.1, s32[2,4,4]{2,1,0:T(4,128)} %adj.1, s32[4]{0:T(128)} %masks.1), custom_call_target="tpu_custom_call" | custom-call | tf_op jit(solution)/shard_map/pallas_call | solution.py:534
  96.6 1.0 copy.9
  97.6 1.0 copy.10

commit v4 on v3

--- a/solution.py
+++ b/solution.py
@@ -291,15 +291,15 @@
         def _():
             (forward(t, c, halo_up, 1) if hop else to_low(t, c, g)).wait_recv()
 
-    def out_start(which, ref, land, c):
+    def out_start(which, ref, land, c, part=slice(None)):
         for k in hops:
             to = lax.rem(me + k, peers)
             pltpu.make_async_remote_copy(
-                src_ref=slab(ref, c, to), dst_ref=piece(land, c, me),
+                src_ref=slab(ref, c, to, part), dst_ref=piece(land, c, me, part),
                 send_sem=out_send.at[which], recv_sem=out_recv.at[which, c // in_band],
                 device_id={"mode": to}, device_id_type=MESH,
             ).start()
-        pltpu.make_async_copy(slab(ref, c, me), piece(land, c, me), own_out.at[which, c // in_band]).start()
+        pltpu.make_async_copy(slab(ref, c, me, part), piece(land, c, me, part), own_out.at[which, c // in_band]).start()
 
     def out_finish(which, land, out, n):
         count = in_band * (peers - 1) * lc
@@ -460,13 +460,13 @@
                 def _():
                     halo_start(t + 1, c, g)
 
+                @pl.when(t == DEGREE - 1)
+                def _():
+                    out_start(1, res, r_land, c, pl.ds(g * per, per))
+
         @pl.when(t == DEGREE - 2)
         def _():
             out_start(0, x.at[last], x_land, c)
-
-        @pl.when(t == DEGREE - 1)
-        def _():
-            out_start(1, res, r_land, c)
 
         @pl.when(t < DEGREE - 1)
         def _():

time: 98.7 us -> 98.2 us (level)
  no operation moved by 1% of the time
where the time goes in v4:
time: 98.2 us; the launch traced here: 98 us
  Pallas kernels  95.4 us (97%)
  local copies, waits for them, and re-layouts  1.94 us (2%)
    pallas_call x1, Pallas kernels, per_device(): pl.pallas_call(functools.partial(solve_kernel, peers, spaces, chunks, mod...  95.4 us

profile of v4, /device:TPU:5, one launch (start us, length us, event | category | flops | bytes accessed | tf_op | source)
XLA Modules:
  0.0 98.0 jit_solution(2555871666438431102)
XLA Ops:
  0.6 95.4 %shard_map.68 = (f32[2,4,128,256]{3,2,1,0:T(8,128)S(1)}, f32[2,4,128,256]{3,2,1,0:T(8,128)S(1)}) custom-call(f32[2,4,128,256]{3,2,1,0:T(8,128)} %source.1, f32[2,4,128,896]{3,2,1,0:T(8,128)} %mean.1, f32[4,2,4,128,896]{4,3,2,1,0:T(8,128)} %fields.1, s32[2,4,4]{2,1,0:T(4,128)} %adj.1, s32[4]{0:T(128)} %masks.1), custom_call_target="tpu_custom_call" | custom-call | tf_op jit(solution)/shard_map/pallas_call | solution.py:534
  96.0 1.0 copy.9
  97.0 1.0 copy.10
